TPU v7x, 128 devices: a whole 4x4x4 slice. The times are simulated.
128 devices in a mesh: row: 16 (over z_hi, y, core), col: 8 (over z_lo, x).
Axes of the slice: x: 4, y: 4, z: 4 (z_hi: 2, z_lo: 2; z = z_hi * 2 + z_lo), core: 2. Of those that a mesh axis runs over, the one named last changes fastest.
Arguments:
- grad_out: bfloat16 [262144, 256], P(('row', 'col')), may hold values from -6 to 6
- preact: bfloat16 [262144, 256], P(('row', 'col')), may hold values from -6 to 6
- features: bfloat16 [262144, 256], P(('col', 'row')), may hold values from -6 to 6
- weight: bfloat16 [256, 256], replicated, may hold values from -0.375 to 0.375
- tiles: bfloat16 [16, 8, 320, 128, 128], P('row', 'col'), may hold values from -0.099609375 to 0.099609375
- tile_rows: int32 [16, 8, 320], P('row', 'col'), may hold values from 0 to 127
- tile_cols: int32 [16, 8, 320], P('row', 'col'), may hold values from 0 to 255
- live_counts: int32 [16, 8], P('row', 'col'), may hold values from 80 to 320, as said below
Outputs:
- grad_features: bfloat16 [262144, 256], P(('col', 'row'))
- grad_weight: float32 [256, 256], replicated
Inputs may be any that keep to these rules, and one draw needn't show every extreme that they name: `live_counts`: some block holds exactly 320 live tiles in every draw.
All inputs are finite; a program needn't handle non-finite values.
Results may differ from a plain program's by a relative error of at most 0.02.
Values may be sent and summed in bfloat16 or wider, within the bound.
A program may use at most 192 MiB of HBM per device.

v0:
```python
import math
import jax
import jax.numpy as jnp
from jax import lax
from jax.sharding import PartitionSpec as P


def body(grad_out, preact, features, weight, tiles, tile_rows, tile_cols, live_counts):
    width = grad_out.shape[1]
    masked = jnp.where(preact > 0, grad_out, jnp.zeros_like(grad_out))
    block = lax.all_gather(masked, "col", axis=0, tiled=True)
    row_count = block.shape[0] // 128
    row_flat = block.reshape(row_count, 128 * width)
    slots = tiles.shape[2]
    tile_stack = tiles.reshape(slots, 128, 128)
    row_index = tile_rows.reshape(slots)
    col_index = tile_cols.reshape(slots)
    count = live_counts.reshape(())
    col_tiles = lax.axis_size("row") * grad_out.shape[0] // 128
    group = math.gcd(slots, 32)
    offsets = jnp.arange(group, dtype=jnp.int32)
    row_ids = jnp.arange(row_count, dtype=jnp.int32)
    col_ids = jnp.arange(col_tiles, dtype=jnp.int32)

    def add_group(step, accum):
        start = step * group
        tile_blk = lax.dynamic_slice_in_dim(tile_stack, start, group, 0)
        rows_now = lax.dynamic_slice_in_dim(row_index, start, group, 0)
        cols_now = lax.dynamic_slice_in_dim(col_index, start, group, 0) - 0
        pick = (rows_now[:, None] == row_ids[None, :]).astype(jnp.bfloat16)
        gathered = jnp.dot(pick, row_flat, preferred_element_type=jnp.float32).astype(jnp.bfloat16)
        gathered = gathered.reshape(group, 128, width)
        prod = jnp.einsum("kab,kaf->kbf", tile_blk, gathered, preferred_element_type=jnp.float32)
        upper = prod.astype(jnp.bfloat16)
        lower = (prod - upper.astype(jnp.float32)).astype(jnp.bfloat16)
        keep = start + offsets < count
        place = ((cols_now[None, :] == col_ids[:, None]) & keep[None, :]).astype(jnp.bfloat16)
        both_place = jnp.concatenate([place, place], axis=1)
        both_vals = jnp.concatenate([upper, lower], axis=0).reshape(2 * group, 128 * width)
        return accum + jnp.dot(both_place, both_vals, preferred_element_type=jnp.float32)

    accum = jnp.zeros((col_tiles, 128 * width), jnp.float32)
    accum = lax.fori_loop(0, slots // group, add_group, accum)
    partial_value = accum.reshape(col_tiles * 128, width)
    summed = lax.psum_scatter(
        partial_value.astype(jnp.bfloat16), "row", scatter_dimension=0, tiled=True
    )
    grad_features = lax.dot_general(
        summed, weight, (((1,), (1,)), ((), ())), preferred_element_type=jnp.float32
    ).astype(jnp.bfloat16)
    weight_term = lax.dot_general(
        features, summed, (((0,), (0,)), ((), ())), preferred_element_type=jnp.float32
    )
    grad_weight = lax.psum(weight_term, ("row", "col"))
    return (grad_features, grad_weight)


def solution(mesh):
    in_specs = (
        P(("row", "col"), None),
        P(("row", "col"), None),
        P(("col", "row"), None),
        P(),
        P("row", "col", None, None, None),
        P("row", "col", None),
        P("row", "col", None),
        P("row", "col"),
    )
    out_specs = (P(("col", "row"), None), P())
    return jax.shard_map(body, mesh=mesh, in_specs=in_specs, out_specs=out_specs, check_vma=False)
```

profile of v0, /device:TPU:1, one launch (start us, length us, event | category | flops | bytes accessed | tf_op | source)
XLA Modules:
  0.0 803.8 jit_solution(6973166508205975980)
XLA Ops:
  7.2 2.7 compare_select_fusion
  10.1 14.5 %copy.12 = bf16[1,1,320,128,128]{3,4,2,1,0:T(8,128)(2,1)} copy(bf16[1,1,320,128,128]{4,3,2,1,0:T(8,128)(2,1)} %param.14) | data formatting | bytes 20971520 | tf_op args[4]
  24.6 80.9 %all-gather.2.cloned.1.call-done = bf16[16384,256]{1,0:T(8,128)(2,1)} async-done(((bf16[2048,256]{1,0:T(8,128)(2,1)}), bf16[16384,256]{1,0:T(8,128)(2,1)}) %all-gather.2.cloned.1.call-update) | async-done | bytes 8388624 | tf_op jit(solution)/shard_map/all_gather | solution.py:11
  105.4 13.4 %reshape.49 = bf16[128,32768]{1,0:T(8,128)(2,1)} reshape(bf16[16384,256]{1,0:T(8,128)(2,1)} %all-gather.2.cloned.1.call-done) | data formatting | bytes 16777216 | tf_op jit(solution)/shard_map/reshape | solution.py:13
  118.9 342.9 %while.14 = (s32[]{:T(128)}, f32[256,32768]{1,0:T(8,128)}, s32[320]{0:T(512)S(1)}, s32[]{:T(128)}, bf16[320,128,128]{1,2,0:T(8,128)(2,1)}, /*index=5*/s32[320]{0...) while((s32[]{:T(128)}, f32[256,32768]{1,0:T(8,128)}, ...), condition=%wide.region_1.2_spmd.clone, body=%wide.region_0.1_spmd.clone.sunk | while | flops 1634766848 | bytes 110117888 | solution.py:43
  119.8 4.6 convolution_convert_fusion.3
  127.3 2.6 copy.19
  129.8 12.4 %convolution_add_fusion.2 = f32[256,32768]{1,0:T(8,128)} fusion(bf16[64,32768]{1,0:T(8,128)(2,1)S(1)} %bitcast.29, f32[256,32768]{1,0:T(8,128)} %get-tuple-element.281, pred[]{:T(512)S(6)} %compare.3, pred[256,32]{0,1:T(32,128)(4,1)S(1)} %fusion.34), kind=kOutput, calls=%fused_computation.3.clone.1 | convolution fusion | flops 1090535424 | bytes 71311360 | tf_op jit(solution)/shard_map/while/body/eval_jaxpr/dot_general | solution.py:40
  143.2 4.6 convolution_convert_fusion.3
  153.2 24.6 %convolution_add_fusion.2 = f32[256,32768]{1,0:T(8,128)} fusion(bf16[64,32768]{1,0:T(8,128)(2,1)S(1)} %bitcast.29, f32[256,32768]{1,0:T(8,128)} %get-tuple-element.281, pred[]{:T(512)S(6)} %compare.3, pred[256,32]{0,1:T(32,128)(4,1)S(1)} %fusion.34), kind=kOutput, calls=%fused_computation.3.clone.1 | convolution fusion | flops 1090535424 | bytes 71311360 | tf_op jit(solution)/shard_map/while/body/eval_jaxpr/dot_general | solution.py:40
  178.7 4.6 convolution_convert_fusion.3
  186.1 2.6 copy.19
  188.7 24.6 %convolution_add_fusion.2 = f32[256,32768]{1,0:T(8,128)} fusion(bf16[64,32768]{1,0:T(8,128)(2,1)S(1)} %bitcast.29, f32[256,32768]{1,0:T(8,128)} %get-tuple-element.281, pred[]{:T(512)S(6)} %compare.3, pred[256,32]{0,1:T(32,128)(4,1)S(1)} %fusion.34), kind=kOutput, calls=%fused_computation.3.clone.1 | convolution fusion | flops 1090535424 | bytes 71311360 | tf_op jit(solution)/shard_map/while/body/eval_jaxpr/dot_general | solution.py:40
  214.2 4.6 convolution_convert_fusion.3
  224.2 24.6 %convolution_add_fusion.2 = f32[256,32768]{1,0:T(8,128)} fusion(bf16[64,32768]{1,0:T(8,128)(2,1)S(1)} %bitcast.29, f32[256,32768]{1,0:T(8,128)} %get-tuple-element.281, pred[]{:T(512)S(6)} %compare.3, pred[256,32]{0,1:T(32,128)(4,1)S(1)} %fusion.34), kind=kOutput, calls=%fused_computation.3.clone.1 | convolution fusion | flops 1090535424 | bytes 71311360 | tf_op jit(solution)/shard_map/while/body/eval_jaxpr/dot_general | solution.py:40
  249.7 4.6 convolution_convert_fusion.3
  259.7 24.6 %convolution_add_fusion.2 = f32[256,32768]{1,0:T(8,128)} fusion(bf16[64,32768]{1,0:T(8,128)(2,1)S(1)} %bitcast.29, f32[256,32768]{1,0:T(8,128)} %get-tuple-element.281, pred[]{:T(512)S(6)} %compare.3, pred[256,32]{0,1:T(32,128)(4,1)S(1)} %fusion.34), kind=kOutput, calls=%fused_computation.3.clone.1 | convolution fusion | flops 1090535424 | bytes 71311360 | tf_op jit(solution)/shard_map/while/body/eval_jaxpr/dot_general | solution.py:40
  285.2 4.6 convolution_convert_fusion.3
  295.2 24.6 %convolution_add_fusion.2 = f32[256,32768]{1,0:T(8,128)} fusion(bf16[64,32768]{1,0:T(8,128)(2,1)S(1)} %bitcast.29, f32[256,32768]{1,0:T(8,128)} %get-tuple-element.281, pred[]{:T(512)S(6)} %compare.3, pred[256,32]{0,1:T(32,128)(4,1)S(1)} %fusion.34), kind=kOutput, calls=%fused_computation.3.clone.1 | convolution fusion | flops 1090535424 | bytes 71311360 | tf_op jit(solution)/shard_map/while/body/eval_jaxpr/dot_general | solution.py:40
  320.7 4.6 convolution_convert_fusion.3
  330.7 24.6 %convolution_add_fusion.2 = f32[256,32768]{1,0:T(8,128)} fusion(bf16[64,32768]{1,0:T(8,128)(2,1)S(1)} %bitcast.29, f32[256,32768]{1,0:T(8,128)} %get-tuple-element.281, pred[]{:T(512)S(6)} %compare.3, pred[256,32]{0,1:T(32,128)(4,1)S(1)} %fusion.34), kind=kOutput, calls=%fused_computation.3.clone.1 | convolution fusion | flops 1090535424 | bytes 71311360 | tf_op jit(solution)/shard_map/while/body/eval_jaxpr/dot_general | solution.py:40
  356.2 4.6 convolution_convert_fusion.3
  366.2 24.6 %convolution_add_fusion.2 = f32[256,32768]{1,0:T(8,128)} fusion(bf16[64,32768]{1,0:T(8,128)(2,1)S(1)} %bitcast.29, f32[256,32768]{1,0:T(8,128)} %get-tuple-element.281, pred[]{:T(512)S(6)} %compare.3, pred[256,32]{0,1:T(32,128)(4,1)S(1)} %fusion.34), kind=kOutput, calls=%fused_computation.3.clone.1 | convolution fusion | flops 1090535424 | bytes 71311360 | tf_op jit(solution)/shard_map/while/body/eval_jaxpr/dot_general | solution.py:40
  391.7 4.6 convolution_convert_fusion.3
  401.7 24.6 %convolution_add_fusion.2 = f32[256,32768]{1,0:T(8,128)} fusion(bf16[64,32768]{1,0:T(8,128)(2,1)S(1)} %bitcast.29, f32[256,32768]{1,0:T(8,128)} %get-tuple-element.281, pred[]{:T(512)S(6)} %compare.3, pred[256,32]{0,1:T(32,128)(4,1)S(1)} %fusion.34), kind=kOutput, calls=%fused_computation.3.clone.1 | convolution fusion | flops 1090535424 | bytes 71311360 | tf_op jit(solution)/shard_map/while/body/eval_jaxpr/dot_general | solution.py:40
  427.2 4.6 convolution_convert_fusion.3
  437.2 24.6 %convolution_add_fusion.2 = f32[256,32768]{1,0:T(8,128)} fusion(bf16[64,32768]{1,0:T(8,128)(2,1)S(1)} %bitcast.29, f32[256,32768]{1,0:T(8,128)} %get-tuple-element.281, pred[]{:T(512)S(6)} %compare.3, pred[256,32]{0,1:T(32,128)(4,1)S(1)} %fusion.34), kind=kOutput, calls=%fused_computation.3.clone.1 | convolution fusion | flops 1090535424 | bytes 71311360 | tf_op jit(solution)/shard_map/while/body/eval_jaxpr/dot_general | solution.py:40
  461.8 17.1 %convert_element_type.45 = bf16[256,32768]{1,0:T(8,128)(2,1)} convert(f32[256,32768]{1,0:T(8,128)} %get-tuple-element.171) | non-fusion elementwise | flops 8388608 | bytes 50331648 | tf_op jit(solution)/shard_map/convert_element_type | solution.py:46
  478.9 25.6 %convert_element_type.46 = bf16[32768,256]{1,0:T(8,128)(2,1)} reshape(bf16[256,32768]{1,0:T(8,128)(2,1)} %convert_element_type.45) | data formatting | bytes 33554432 | tf_op jit(solution)/shard_map/convert_element_type | solution.py:46
  504.6 145.1 %reduce-scatter.2.cloned.1.call-done = bf16[2048,256]{1,0:T(8,128)(2,1)} async-done(((bf16[32768,256]{1,0:T(8,128)(2,1)}), bf16[2048,256]{1,0:T(8,128)(2,1)}) %reduce-scatter.2.cloned.1.call-update) | async-done | bytes 1048592 | tf_op jit(solution)/shard_map/reduce_scatter | solution.py:45
  652.1 2.7 convolution_convert_fusion.1
  654.8 140.8 %all-reduce.2.cloned.1.call-done = f32[256,256]{0,1:T(8,128)} async-done(((f32[256,256]{0,1:T(8,128)}), f32[256,256]{0,1:T(8,128)}) %all-reduce.2.cloned.1.call-update) | async-done | bytes 262160 | tf_op jit(solution)/shard_map/psum | solution.py:54
  (97 shorter events, 61.7 us)
Async XLA Ops:
  7.2 642.5 %copy-start = (bf16[2048,256]{1,0:T(8,128)(2,1)S(1)}, bf16[2048,256]{1,0:T(8,128)(2,1)}, u32[]{:S(2)}) copy-start(bf16[2048,256]{1,0:T(8,128)(2,1)} %param.12) | copy-start | bytes 3145732
  7.2 2.9 copy-start.2
  7.2 2.9 copy-start.3
  7.2 98.2 %all-gather.2.cloned.1.call-start = ((), (), s32[]{:S(2)}) async-start(), calls=%async_computation.1 | async-start | bytes 9437184 | tf_op jit(solution)/shard_map/all_gather | solution.py:11
  10.0 639.7 %reduce-scatter.2.cloned.1.call-start = ((), (), s32[]{:S(2)}) async-start(), calls=%async_computation.2 | async-start | bytes 17825792 | tf_op jit(solution)/shard_map/reduce_scatter | solution.py:45
  504.5 147.6 %copy-start.1 = (bf16[256,256]{1,0:T(8,128)(2,1)S(1)}, bf16[256,256]{1,0:T(8,128)(2,1)}, u32[]{:S(2)}) copy-start(bf16[256,256]{1,0:T(8,128)(2,1)} %param.13) | copy-start | bytes 393220
  504.6 291.0 %all-reduce.2.cloned.1.call-start = ((), (), s32[]{:S(2)}) async-start(), calls=%async_computation.3 | async-start | bytes 524288 | tf_op jit(solution)/shard_map/psum | solution.py:54
Sparse Core Ops, SparseCore 0:
  10.3 95.1 all-gather.1
  504.7 144.9 reduce-scatter.1
  655.7 139.7 all-reduce.1
where the time goes:
time: 806 us; the launch traced here: 804 us
  waiting for transfers between devices  367 us (46%)
  matrix products  304 us (38%)
  local copies, waits for them, and re-layouts  87.5 us (11%)
  other arithmetic  30.8 us (4%)
  between operations  13.8 us (2%)
    dot_general x10, matrix products, add_group(): jnp.dot(both_place, both_vals, preferred_element_type=jnp.float32)  234 us
    reduce_scatter x1, waiting for transfers between devices, body(): lax.psum_scatter(partial_value.astype(jnp.bfloat16), 'row', scatter_dimen...  145 us
    psum x1, waiting for transfers between devices, body(): grad_weight = lax.psum(weight_term, ('row', 'col'))  141 us
    all_gather x1, waiting for transfers between devices, body(): block = lax.all_gather(masked, 'col', axis=0, tiled=True)  80.9 us
    dot_general x10, matrix products, add_group(): jnp.dot(pick, row_flat, preferred_element_type=jnp.float32)  46.4 us
    while x20, local copies, waits for them, and re-layouts  30.6 us
    convert_element_type x1, local copies, waits for them, and re-layouts, body(): partial_value.astype(jnp.bfloat16)  25.6 us
    dot_general x10, matrix products, add_group(): jnp.einsum('kab,kaf->kbf', tile_blk, gathered, preferred_element_type=jnp...  19.4 us
  transfers between devices with their start and end apart: 3, of which 3 were waited for; matrix products, arithmetic and copies ran while one was open for 2% of the time, Pallas kernels for 0%

commit v1 on v0

--- a/solution.py
+++ b/solution.py
@@ -8,7 +8,9 @@
 def body(grad_out, preact, features, weight, tiles, tile_rows, tile_cols, live_counts):
     width = grad_out.shape[1]
     masked = jnp.where(preact > 0, grad_out, jnp.zeros_like(grad_out))
-    block = lax.all_gather(masked, "col", axis=0, tiled=True)
+    block = jnp.concatenate(
+        lax.all_to_all(jnp.stack([masked] * lax.axis_size("col")), "col", 0, 0), axis=0
+    )
     row_count = block.shape[0] // 128
     row_flat = block.reshape(row_count, 128 * width)
     slots = tiles.shape[2]

time: 806 us -> 848 us (1.052)
  waiting for transfers between devices: 367 us -> 399 us
    all_gather x1 -> x0, waiting for transfers between devices: 80.9 us -> none  [body(): block = lax.all_gather(masked, 'col', axis=0, tiled=True)]
    all_to_all x0 -> x1, waiting for transfers between devices: none -> 80.1 us  [body(): lax.all_to_all(jnp.stack([masked] * lax.axis_size('col')), 'col', 0, 0)]
    reduce_scatter x1, waiting for transfers between devices: 145 us -> 178 us  [body(): lax.psum_scatter(partial_value.astype(jnp.bfloat16), 'row', scatter_dimen...]
    another operation x0 -> x2, local copies, waits for them, and re-layouts: none -> 17.3 us  [the longest x1 13.5 us: body(): row_flat = block.reshape(row_count, 128 * width)]
    reshape x1 -> x0, local copies, waits for them, and re-layouts: 13.4 us -> none  [body(): row_flat = block.reshape(row_count, 128 * width)]
where the time goes in v1:
time: 848 us; the launch traced here: 846 us
  waiting for transfers between devices  399 us (47%)
  matrix products  305 us (36%)
  local copies, waits for them, and re-layouts  91.2 us (11%)
  other arithmetic  29.8 us (4%)
  between operations  14.1 us (2%)
    dot_general x10, matrix products, add_group(): jnp.dot(both_place, both_vals, preferred_element_type=jnp.float32)  234 us
    reduce_scatter x1, waiting for transfers between devices, body(): lax.psum_scatter(partial_value.astype(jnp.bfloat16), 'row', scatter_dimen...  178 us
    psum x1, waiting for transfers between devices, body(): grad_weight = lax.psum(weight_term, ('row', 'col'))  141 us
    all_to_all x1, waiting for transfers between devices, body(): lax.all_to_all(jnp.stack([masked] * lax.axis_size('col')), 'col', 0, 0)  80.1 us
    dot_general x10, matrix products, add_group(): jnp.dot(pick, row_flat, preferred_element_type=jnp.float32)  46.4 us
    while x20, local copies, waits for them, and re-layouts  30.6 us
    convert_element_type x1, local copies, waits for them, and re-layouts, body(): partial_value.astype(jnp.bfloat16)  25.6 us
    dot_general x10, matrix products, add_group(): jnp.einsum('kab,kaf->kbf', tile_blk, gathered, preferred_element_type=jnp...  19.4 us
  transfers between devices with their start and end apart: 3, of which 3 were waited for; matrix products, arithmetic and copies ran while one was open for 2% of the time, Pallas kernels for 0%

profile of v1, /device:TPU:1, one launch (start us, length us, event | category | flops | bytes accessed | tf_op | source)
XLA Modules:
  0.0 845.7 jit_solution(4987231107171652965)
XLA Ops:
  8.9 3.8 stack.2
  12.8 6.3 all-to-all-start
  19.2 14.4 %copy.12 = bf16[1,1,320,128,128]{3,4,2,1,0:T(8,128)(2,1)} copy(bf16[1,1,320,128,128]{4,3,2,1,0:T(8,128)(2,1)} %param.14) | data formatting | bytes 20971520 | tf_op args[4]
  33.6 80.1 %all-to-all-done = bf16[8,2048,256]{2,1,0:T(8,128)(2,1)} async-done(((bf16[8,2048,256]{2,1,0:T(8,128)(2,1)}), bf16[8,2048,256]{2,1,0:T(8,128)(2,1)}, u32[]{:S(2)}, u32[]{:S(2)}) %all-to-all-start) | async-done | bytes 8388640 | tf_op jit(solution)/shard_map/all_to_all | solution.py:12
  113.7 13.5 %reshape_reshape.3 = bf16[128,32768]{1,0:T(8,128)(2,1)} reshape(bf16[8,2048,256]{2,1,0:T(8,128)(2,1)} %all-to-all-done) | data formatting | bytes 16777216 | tf_op jit(solution)/shard_map/reshape;reshape | solution.py:15
  127.1 343.1 %while.14 = (s32[]{:T(128)}, f32[256,32768]{1,0:T(8,128)}, s32[320]{0:T(512)S(1)}, s32[]{:T(128)}, bf16[320,128,128]{1,2,0:T(8,128)(2,1)}, /*index=5*/s32[320]{0...) while((s32[]{:T(128)}, f32[256,32768]{1,0:T(8,128)}, ...), condition=%wide.region_1.2_spmd.clone, body=%wide.region_0.1_spmd.clone.sunk | while | flops 1634766848 | bytes 110117888 | solution.py:45
  128.0 4.6 convolution_convert_fusion.3
  135.5 2.6 copy.19
  138.1 12.4 %convolution_add_fusion.2 = f32[256,32768]{1,0:T(8,128)} fusion(bf16[64,32768]{1,0:T(8,128)(2,1)S(1)} %bitcast.29, f32[256,32768]{1,0:T(8,128)} %get-tuple-element.281, pred[]{:T(512)S(6)} %compare.3, pred[256,32]{0,1:T(32,128)(4,1)S(1)} %fusion.34), kind=kOutput, calls=%fused_computation.3.clone.1 | convolution fusion | flops 1090535424 | bytes 71311360 | tf_op jit(solution)/shard_map/while/body/eval_jaxpr/dot_general | solution.py:42
  151.4 4.6 convolution_convert_fusion.3
  161.4 24.6 %convolution_add_fusion.2 = f32[256,32768]{1,0:T(8,128)} fusion(bf16[64,32768]{1,0:T(8,128)(2,1)S(1)} %bitcast.29, f32[256,32768]{1,0:T(8,128)} %get-tuple-element.281, pred[]{:T(512)S(6)} %compare.3, pred[256,32]{0,1:T(32,128)(4,1)S(1)} %fusion.34), kind=kOutput, calls=%fused_computation.3.clone.1 | convolution fusion | flops 1090535424 | bytes 71311360 | tf_op jit(solution)/shard_map/while/body/eval_jaxpr/dot_general | solution.py:42
  186.9 4.6 convolution_convert_fusion.3
  197.0 24.6 %convolution_add_fusion.2 = f32[256,32768]{1,0:T(8,128)} fusion(bf16[64,32768]{1,0:T(8,128)(2,1)S(1)} %bitcast.29, f32[256,32768]{1,0:T(8,128)} %get-tuple-element.281, pred[]{:T(512)S(6)} %compare.3, pred[256,32]{0,1:T(32,128)(4,1)S(1)} %fusion.34), kind=kOutput, calls=%fused_computation.3.clone.1 | convolution fusion | flops 1090535424 | bytes 71311360 | tf_op jit(solution)/shard_map/while/body/eval_jaxpr/dot_general | solution.py:42
  222.5 4.6 convolution_convert_fusion.3
  232.5 24.6 %convolution_add_fusion.2 = f32[256,32768]{1,0:T(8,128)} fusion(bf16[64,32768]{1,0:T(8,128)(2,1)S(1)} %bitcast.29, f32[256,32768]{1,0:T(8,128)} %get-tuple-element.281, pred[]{:T(512)S(6)} %compare.3, pred[256,32]{0,1:T(32,128)(4,1)S(1)} %fusion.34), kind=kOutput, calls=%fused_computation.3.clone.1 | convolution fusion | flops 1090535424 | bytes 71311360 | tf_op jit(solution)/shard_map/while/body/eval_jaxpr/dot_general | solution.py:42
  258.0 4.6 convolution_convert_fusion.3
  268.0 24.6 %convolution_add_fusion.2 = f32[256,32768]{1,0:T(8,128)} fusion(bf16[64,32768]{1,0:T(8,128)(2,1)S(1)} %bitcast.29, f32[256,32768]{1,0:T(8,128)} %get-tuple-element.281, pred[]{:T(512)S(6)} %compare.3, pred[256,32]{0,1:T(32,128)(4,1)S(1)} %fusion.34), kind=kOutput, calls=%fused_computation.3.clone.1 | convolution fusion | flops 1090535424 | bytes 71311360 | tf_op jit(solution)/shard_map/while/body/eval_jaxpr/dot_general | solution.py:42
  293.5 4.6 convolution_convert_fusion.3
  303.5 24.6 %convolution_add_fusion.2 = f32[256,32768]{1,0:T(8,128)} fusion(bf16[64,32768]{1,0:T(8,128)(2,1)S(1)} %bitcast.29, f32[256,32768]{1,0:T(8,128)} %get-tuple-element.281, pred[]{:T(512)S(6)} %compare.3, pred[256,32]{0,1:T(32,128)(4,1)S(1)} %fusion.34), kind=kOutput, calls=%fused_computation.3.clone.1 | convolution fusion | flops 1090535424 | bytes 71311360 | tf_op jit(solution)/shard_map/while/body/eval_jaxpr/dot_general | solution.py:42
  329.0 4.6 convolution_convert_fusion.3
  339.1 24.6 %convolution_add_fusion.2 = f32[256,32768]{1,0:T(8,128)} fusion(bf16[64,32768]{1,0:T(8,128)(2,1)S(1)} %bitcast.29, f32[256,32768]{1,0:T(8,128)} %get-tuple-element.281, pred[]{:T(512)S(6)} %compare.3, pred[256,32]{0,1:T(32,128)(4,1)S(1)} %fusion.34), kind=kOutput, calls=%fused_computation.3.clone.1 | convolution fusion | flops 1090535424 | bytes 71311360 | tf_op jit(solution)/shard_map/while/body/eval_jaxpr/dot_general | solution.py:42
  364.6 4.6 convolution_convert_fusion.3
  374.6 24.6 %convolution_add_fusion.2 = f32[256,32768]{1,0:T(8,128)} fusion(bf16[64,32768]{1,0:T(8,128)(2,1)S(1)} %bitcast.29, f32[256,32768]{1,0:T(8,128)} %get-tuple-element.281, pred[]{:T(512)S(6)} %compare.3, pred[256,32]{0,1:T(32,128)(4,1)S(1)} %fusion.34), kind=kOutput, calls=%fused_computation.3.clone.1 | convolution fusion | flops 1090535424 | bytes 71311360 | tf_op jit(solution)/shard_map/while/body/eval_jaxpr/dot_general | solution.py:42
  400.1 4.6 convolution_convert_fusion.3
  410.1 24.6 %convolution_add_fusion.2 = f32[256,32768]{1,0:T(8,128)} fusion(bf16[64,32768]{1,0:T(8,128)(2,1)S(1)} %bitcast.29, f32[256,32768]{1,0:T(8,128)} %get-tuple-element.281, pred[]{:T(512)S(6)} %compare.3, pred[256,32]{0,1:T(32,128)(4,1)S(1)} %fusion.34), kind=kOutput, calls=%fused_computation.3.clone.1 | convolution fusion | flops 1090535424 | bytes 71311360 | tf_op jit(solution)/shard_map/while/body/eval_jaxpr/dot_general | solution.py:42
  435.6 4.6 convolution_convert_fusion.3
  445.6 24.6 %convolution_add_fusion.2 = f32[256,32768]{1,0:T(8,128)} fusion(bf16[64,32768]{1,0:T(8,128)(2,1)S(1)} %bitcast.29, f32[256,32768]{1,0:T(8,128)} %get-tuple-element.281, pred[]{:T(512)S(6)} %compare.3, pred[256,32]{0,1:T(32,128)(4,1)S(1)} %fusion.34), kind=kOutput, calls=%fused_computation.3.clone.1 | convolution fusion | flops 1090535424 | bytes 71311360 | tf_op jit(solution)/shard_map/while/body/eval_jaxpr/dot_general | solution.py:42
  470.2 17.1 %convert_element_type.45 = bf16[256,32768]{1,0:T(8,128)(2,1)} convert(f32[256,32768]{1,0:T(8,128)} %get-tuple-element.171) | non-fusion elementwise | flops 8388608 | bytes 50331648 | tf_op jit(solution)/shard_map/convert_element_type | solution.py:48
  487.4 25.6 %convert_element_type.46 = bf16[32768,256]{1,0:T(8,128)(2,1)} reshape(bf16[256,32768]{1,0:T(8,128)(2,1)} %convert_element_type.45) | data formatting | bytes 33554432 | tf_op jit(solution)/shard_map/convert_element_type | solution.py:48
  513.1 178.1 %reduce-scatter.2.cloned.1.call-done = bf16[2048,256]{1,0:T(8,128)(2,1)} async-done(((bf16[32768,256]{1,0:T(8,128)(2,1)}), bf16[2048,256]{1,0:T(8,128)(2,1)}) %reduce-scatter.2.cloned.1.call-update) | async-done | bytes 1048592 | tf_op jit(solution)/shard_map/reduce_scatter | solution.py:47
  693.6 2.7 convolution_convert_fusion.1
  696.3 140.7 %all-reduce.2.cloned.1.call-done = f32[256,256]{0,1:T(8,128)} async-done(((f32[256,256]{0,1:T(8,128)}), f32[256,256]{0,1:T(8,128)}) %all-reduce.2.cloned.1.call-update) | async-done | bytes 262160 | tf_op jit(solution)/shard_map/psum | solution.py:56
  (97 shorter events, 66.0 us)
Async XLA Ops:
  7.2 684.0 %copy-start = (bf16[2048,256]{1,0:T(8,128)(2,1)S(1)}, bf16[2048,256]{1,0:T(8,128)(2,1)}, u32[]{:S(2)}) copy-start(bf16[2048,256]{1,0:T(8,128)(2,1)} %param.12) | copy-start | bytes 3145732
  12.8 6.4 copy-start.2
  12.8 6.4 copy-start.3
  12.8 100.9 %all-to-all-start = ((bf16[8,2048,256]{2,1,0:T(8,128)(2,1)}), bf16[8,2048,256]{2,1,0:T(8,128)(2,1)}, u32[]{:S(2)}, u32[]{:S(2)}) async-start(bf16[8,2048,256]{2,1,0:T(8,128)(2,1)} %stack.2), calls=%async_computation | async-start | bytes 16777216 | tf_op jit(solution)/shard_map/all_to_all | solution.py:12
  19.1 672.1 %reduce-scatter.2.cloned.1.call-start = ((), (), s32[]{:S(2)}) async-start(), calls=%async_computation.2 | async-start | bytes 17825792 | tf_op jit(solution)/shard_map/reduce_scatter | solution.py:47
  513.0 180.6 %copy-start.1 = (bf16[256,256]{1,0:T(8,128)(2,1)S(1)}, bf16[256,256]{1,0:T(8,128)(2,1)}, u32[]{:S(2)}) copy-start(bf16[256,256]{1,0:T(8,128)(2,1)} %param.13) | copy-start | bytes 393220
  513.0 324.0 %all-reduce.2.cloned.1.call-start = ((), (), s32[]{:S(2)}) async-start(), calls=%async_computation.3 | async-start | bytes 524288 | tf_op jit(solution)/shard_map/psum | solution.py:56
Sparse Core Ops, SparseCore 0:
  513.1 178.0 reduce-scatter.1
  697.2 139.7 all-reduce.1
